TPU v7x, 32 devices: a whole 2x2x4 slice. The times are simulated.
32 devices in a mesh: grp: 4 (over y, core), blk: 8 (over z, x).
Axes of the slice: x: 2, y: 2, z: 4, core: 2. Of those that a mesh axis runs over, the one named last changes fastest.
Arguments:
- features: bfloat16 [4096, 128], P(('grp', 'blk')), may hold values from -6 to 6
- col_scale: float32 [4096], P(('grp', 'blk')), may hold values from 0.5 to 2
- row_scale: float32 [4096], P(('grp', 'blk')), may hold values from 0.5 to 2
- tiles: bfloat16 [1024, 128, 128], P(('grp', 'blk')), may hold values from 0 to 0.03125
- tile_cols: int32 [1024], P(('grp', 'blk')), may hold values from 0 to 3
- weight: bfloat16 [128, 256], replicated, may hold values from -0.5 to 0.5
- cotangent: bfloat16 [4096, 256], P(('grp', 'blk')), may hold values from -0.1875 to 0.1875
- train_mask: int32 [4096], P(('grp', 'blk')), may hold values 0 or 1
Outputs:
- hidden: bfloat16 [4096, 256], P(('grp', 'blk'))
- weight_grad: float32 [128, 256], replicated
All inputs are finite; a program needn't handle non-finite values. No bound on the sum of `train_mask` on one device may be relied on, other than what follows from the above.
Results may differ from a plain program's by a relative error of at most 0.0054.
Values may be sent and summed in bfloat16 or wider, within the bound.
A program may use at most 128 MiB of HBM per device.

v0:
```python
import jax
import jax.numpy as jnp
from jax import lax
from jax.sharding import PartitionSpec as P

TPR = 4


def activate(values):
    return jax.nn.gelu(values, approximate=True)


def shards(features, col_scale, row_scale, tiles, tile_cols, weight, cotangent, train_mask):
    node_dev = features.shape[0]
    fin_width = features.shape[1]
    tile = tiles.shape[1]
    per_dev = node_dev // tile
    grp_count = lax.axis_size("grp")
    blk_count = lax.axis_size("blk")
    scaled = (col_scale[:, None] * features.astype(jnp.float32)).astype(jnp.bfloat16)
    moved_tiles, moved_cols = (
        lax.all_to_all(tiles, "blk", split_axis=0, concat_axis=0, tiled=True),
        lax.all_to_all(tile_cols, "blk", split_axis=0, concat_axis=0, tiled=True),
    )
    everything = lax.all_gather(scaled, ("grp", "blk"), axis=0, tiled=True)
    everything = everything.reshape(grp_count * blk_count * per_dev, tile, fin_width)
    cols_view = moved_cols.reshape(blk_count, per_dev * TPR)
    colset = jnp.arange(blk_count, dtype=jnp.int32)[:, None]
    global_cols = (cols_view // per_dev * blk_count + colset) * per_dev + cols_view % per_dev
    picked = jnp.take(everything, global_cols.reshape(-1), axis=0)
    picked = picked.reshape(blk_count, per_dev, TPR, tile, fin_width)
    piece = moved_tiles.reshape(blk_count, per_dev, TPR, tile, tile)
    aggregate = jnp.einsum("bpkij,bpkjf->pif", piece, picked, preferred_element_type=jnp.float32)
    aggregate = aggregate.reshape(node_dev, fin_width)
    mixed = row_scale[:, None] * aggregate
    pre = jnp.dot(mixed, weight.astype(jnp.float32), precision=lax.Precision.HIGHEST)
    hidden, backward = jax.vjp(activate, pre)
    masked_grad = cotangent.astype(jnp.float32) * train_mask.astype(jnp.float32)[:, None]
    delta = backward(masked_grad)[0]
    local_grad = jnp.dot(mixed.T, delta, precision=lax.Precision.HIGHEST)
    weight_grad = lax.psum(local_grad, ("grp", "blk"))
    return (hidden.astype(jnp.bfloat16), weight_grad)


def solution(mesh):
    in_specs = (
        P(("grp", "blk"), None),
        P(("grp", "blk")),
        P(("grp", "blk")),
        P(("grp", "blk"), None, None),
        P(("grp", "blk")),
        P(),
        P(("grp", "blk"), None),
        P(("grp", "blk")),
    )
    out_specs = (P(("grp", "blk"), None), P())
    return jax.shard_map(shards, mesh=mesh, in_specs=in_specs, out_specs=out_specs, check_vma=False)
```

profile of v0, /device:TPU:0, one launch (start us, length us, event | category | flops | bytes accessed | tf_op | source)
XLA Modules:
  0.0 208.8 jit_solution(1757387805213414297)
XLA Ops:
  7.2 0.0 copy-start
  7.2 0.0 all-gather.2.cloned.1.call-start
  7.2 1.5 multiply_convert_fusion.1
  8.7 0.0 copy-start.1
  8.7 0.0 all-gather.2.cloned.1.call-update
  8.7 0.6 copy-done.1
  9.3 0.1 all_to_all.9
  9.4 13.5 %all_to_all.14 = s32[8,4,1]{1,2,0:T(1,128)S(1)} all-to-all(s32[8,4,1]{1,2,0:T(1,128)S(1)} %bitcast.25), channel_id=1, replica_groups=mesh['grp'=4,'blk'=8] {'blk'}, dimensions={0} | all-to-all | bytes 256 | tf_op jit(solution)/shard_map/all_to_all | solution.py:23
  22.9 3.6 %all-to-all-start.1 = ((bf16[32,128,128]{2,1,0:T(8,128)(2,1)}), bf16[32,128,128]{2,1,0:T(8,128)(2,1)S(1)}, u32[]{:S(2)}, u32[]{:S(2)}) async-start(bf16[32,128,128]{2,1,0:T(8,128)(2,1)} %param.11), calls=%async_computation.1 | async-start | bytes 2097152 | tf_op jit(solution)/shard_map/all_to_all | solution.py:22
  26.5 0.0 all-reduce.2.cloned.1.call-start
  26.6 0.0 copy-start.3
  26.6 0.1 add.82
  26.6 0.6 copy-done.3
  27.2 0.1 mul.98
  27.3 0.1 copy.17
  27.4 0.1 copy.18
  27.5 45.2 %all-gather.2.cloned.1.call-done = bf16[4096,128]{1,0:T(8,128)(2,1)} async-done(((bf16[128,128]{1,0:T(8,128)(2,1)}), bf16[4096,128]{1,0:T(8,128)(2,1)}) %all-gather.2.cloned.1.call-update) | async-done | bytes 1048592 | tf_op jit(solution)/shard_map/all_gather | solution.py:25
  72.8 2.0 gather_fusion
  74.8 0.7 copy.19
  75.4 0.0 all-to-all-done.1
  75.4 0.0 copy-start.4
  75.4 0.6 copy-done.4
  76.1 0.5 fusion
  76.6 0.0 copy-done
  76.6 0.0 copy-start.2
  76.6 0.9 multiply_convert_fusion
  77.5 0.0 copy-done.2
  77.5 1.0 fusion.10
  78.6 0.0 all-reduce.2.cloned.1.call-update
  78.6 121.8 %all-reduce.2.cloned.1.call-done = f32[128,256]{1,0:T(8,128)} async-done(((f32[128,256]{1,0:T(8,128)}), f32[128,256]{1,0:T(8,128)}) %all-reduce.2.cloned.1.call-update) | async-done | bytes 131088 | tf_op jit(solution)/shard_map/psum | solution.py:41
  200.4 1.6 copy.22
  (6 shorter events, 0.0 us)
Async XLA Ops:
  7.2 69.4 %copy-start = (bf16[128,256]{1,0:T(8,128)(2,1)S(1)}, bf16[128,256]{1,0:T(8,128)(2,1)}, u32[]{:S(2)}) copy-start(bf16[128,256]{1,0:T(8,128)(2,1)} %param.13) | copy-start | bytes 196612
  7.2 65.6 %all-gather.2.cloned.1.call-start = ((), (), s32[]{:S(2)}) async-start(), calls=%async_computation.2 | async-start | bytes 1081344 | tf_op jit(solution)/shard_map/all_gather | solution.py:25
  8.7 0.7 copy-start.1
  22.9 52.5 %all-to-all-start.1 = ((bf16[32,128,128]{2,1,0:T(8,128)(2,1)}), bf16[32,128,128]{2,1,0:T(8,128)(2,1)S(1)}, u32[]{:S(2)}, u32[]{:S(2)}) async-start(bf16[32,128,128]{2,1,0:T(8,128)(2,1)} %param.11), calls=%async_computation.1 | async-start | bytes 2097152 | tf_op jit(solution)/shard_map/all_to_all | solution.py:22
  26.5 173.9 %all-reduce.2.cloned.1.call-start = ((), (), s32[]{:S(2)}) async-start(), calls=%async_computation.3 | async-start | bytes 262144 | tf_op jit(solution)/shard_map/psum | solution.py:41
  26.6 0.7 copy-start.3
  75.4 0.7 copy-start.4
  76.6 0.9 copy-start.2
Sparse Core Ops, SparseCore 0:
  11.6 61.1 all-gather.1
  78.9 121.4 all-reduce.1
where the time goes:
time: 209 us
  waiting for transfers between devices  167 us (80%)
  between operations  14.1 us (7%)
  blocking collectives  13.5 us (6%)
  local copies, waits for them, and re-layouts  6.49 us (3%)
  starting transfers between devices  3.64 us (2%)
  matrix products  2.43 us (1%)
    psum x1, waiting for transfers between devices, shards(): weight_grad = lax.psum(local_grad, ('grp', 'blk'))  122 us
    all_gather x1, waiting for transfers between devices, shards(): everything = lax.all_gather(scaled, ('grp', 'blk'), axis=0, tiled=True)  45.2 us
    all_to_all x1, blocking collectives, shards(): lax.all_to_all(tile_cols, 'blk', split_axis=0, concat_axis=0, tiled=True)  13.5 us
  transfers between devices with their start and end apart: 3, of which 2 were waited for; matrix products, arithmetic and copies ran while one was open for 1% of the time, Pallas kernels for 0%

commit v1 on v0

--- a/solution.py
+++ b/solution.py
@@ -38,7 +38,7 @@
     masked_grad = cotangent.astype(jnp.float32) * train_mask.astype(jnp.float32)[:, None]
     delta = backward(masked_grad)[0]
     local_grad = jnp.dot(mixed.T, delta, precision=lax.Precision.HIGHEST)
-    weight_grad = lax.psum(local_grad, ("grp", "blk"))
+    weight_grad = lax.psum(lax.psum(local_grad, "blk"), "grp")
     return (hidden.astype(jnp.bfloat16), weight_grad)
 
 

time: 209 us -> 189 us (0.904)
  waiting for transfers between devices: 167 us -> 147 us
    psum x1 -> x2, waiting for transfers between devices: 122 us -> 102 us  [shards(): weight_grad = lax.psum(lax.psum(local_grad, 'blk'), 'grp')]
  transfers between devices with their start and end apart: 3 -> 4, of which waited for: 2 -> 3; matrix products, arithmetic and copies ran while one was open for 1% -> 2% of each run, Pallas kernels for 0% -> 0%
where the time goes in v1:
time: 189 us
  waiting for transfers between devices  147 us (78%)
  between operations  13.8 us (7%)
  blocking collectives  13.5 us (7%)
  local copies, waits for them, and re-layouts  6.49 us (3%)
  starting transfers between devices  3.68 us (2%)
  matrix products  2.43 us (1%)
    psum x2, waiting for transfers between devices, shards(): weight_grad = lax.psum(lax.psum(local_grad, 'blk'), 'grp')  102 us
    all_gather x1, waiting for transfers between devices, shards(): everything = lax.all_gather(scaled, ('grp', 'blk'), axis=0, tiled=True)  45.2 us
    all_to_all x1, blocking collectives, shards(): lax.all_to_all(tile_cols, 'blk', split_axis=0, concat_axis=0, tiled=True)  13.5 us
  transfers between devices with their start and end apart: 4, of which 3 were waited for; matrix products, arithmetic and copies ran while one was open for 2% of the time, Pallas kernels for 0%

profile of v1, /device:TPU:0, one launch (start us, length us, event | category | flops | bytes accessed | tf_op | source)
XLA Modules:
  0.0 188.7 jit_solution(539398954041927125)
XLA Ops:
  7.2 0.0 copy-start
  7.2 0.0 all-gather.2.cloned.1.call-start
  7.2 1.5 multiply_convert_fusion.1
  8.7 0.0 all-gather.2.cloned.1.call-update
  8.7 0.6 copy-done.1
  9.3 0.1 all_to_all.9
  9.4 13.5 %all_to_all.14 = s32[8,4,1]{1,2,0:T(1,128)S(1)} all-to-all(s32[8,4,1]{1,2,0:T(1,128)S(1)} %bitcast.25), channel_id=1, replica_groups=mesh['grp'=4,'blk'=8] {'blk'}, dimensions={0} | all-to-all | bytes 256 | tf_op jit(solution)/shard_map/all_to_all | solution.py:23
  22.9 3.6 %all-to-all-start.1 = ((bf16[32,128,128]{2,1,0:T(8,128)(2,1)}), bf16[32,128,128]{2,1,0:T(8,128)(2,1)S(1)}, u32[]{:S(2)}, u32[]{:S(2)}) async-start(bf16[32,128,128]{2,1,0:T(8,128)(2,1)} %param.11), calls=%async_computation.1 | async-start | bytes 2097152 | tf_op jit(solution)/shard_map/all_to_all | solution.py:22
  26.5 0.0 all-reduce.3.cloned.1.call-start
  26.6 0.0 copy-start.3
  26.6 0.1 add.84
  26.6 0.6 copy-done.3
  27.2 0.1 mul.98
  27.3 0.1 copy.17
  27.4 0.1 copy.18
  27.5 45.2 %all-gather.2.cloned.1.call-done = bf16[4096,128]{1,0:T(8,128)(2,1)} async-done(((bf16[128,128]{1,0:T(8,128)(2,1)}), bf16[4096,128]{1,0:T(8,128)(2,1)}) %all-gather.2.cloned.1.call-update) | async-done | bytes 1048592 | tf_op jit(solution)/shard_map/all_gather | solution.py:25
  72.8 2.0 %gather_fusion = bf16[32,128,128]{2,1,0:T(8,128)(2,1)S(1)} fusion(bf16[32,128,128]{2,1,0:T(8,128)(2,1)} %bitcast.22, s32[1024]{0:T(1024)S(1)} %pad_clamp_fusion), kind=kCustom, calls=%fused_computation | custom fusion | bytes 2097280 | tf_op jit(solution)/shard_map/jit(_take)/gather | solution.py:30
  74.8 0.7 copy.19
  75.4 0.0 all-to-all-done.1
  75.4 0.0 copy-start.4
  75.4 0.6 copy-done.4
  76.1 0.5 fusion
  76.6 0.0 copy-done
  76.6 0.0 copy-start.2
  76.6 0.9 multiply_convert_fusion
  77.5 1.0 fusion.10
  78.6 0.0 all-reduce.3.cloned.1.call-update
  78.6 0.0 all-reduce.5.cloned.1.call-start
  78.6 68.8 %all-reduce.3.cloned.1.call-done = f32[128,256]{1,0:T(8,128)} async-done(((f32[128,256]{1,0:T(8,128)}), f32[128,256]{1,0:T(8,128)}) %all-reduce.3.cloned.1.call-update) | async-done | bytes 131088 | tf_op jit(solution)/shard_map/psum | solution.py:41
  147.5 0.0 all-reduce.5.cloned.1.call-update
  147.5 33.1 %all-reduce.5.cloned.1.call-done = f32[128,256]{1,0:T(8,128)} async-done(((f32[128,256]{1,0:T(8,128)}), f32[128,256]{1,0:T(8,128)}) %all-reduce.5.cloned.1.call-update) | async-done | bytes 131088 | tf_op jit(solution)/shard_map/psum | solution.py:41
  180.6 1.6 copy.23
  (8 shorter events, 0.1 us)
Async XLA Ops:
  7.2 69.4 %copy-start = (bf16[128,256]{1,0:T(8,128)(2,1)S(1)}, bf16[128,256]{1,0:T(8,128)(2,1)}, u32[]{:S(2)}) copy-start(bf16[128,256]{1,0:T(8,128)(2,1)} %param.13) | copy-start | bytes 196612
  7.2 65.6 %all-gather.2.cloned.1.call-start = ((), (), s32[]{:S(2)}) async-start(), calls=%async_computation.2 | async-start | bytes 1081344 | tf_op jit(solution)/shard_map/all_gather | solution.py:25
  8.7 0.7 copy-start.1
  22.9 52.5 %all-to-all-start.1 = ((bf16[32,128,128]{2,1,0:T(8,128)(2,1)}), bf16[32,128,128]{2,1,0:T(8,128)(2,1)S(1)}, u32[]{:S(2)}, u32[]{:S(2)}) async-start(bf16[32,128,128]{2,1,0:T(8,128)(2,1)} %param.11), calls=%async_computation.1 | async-start | bytes 2097152 | tf_op jit(solution)/shard_map/all_to_all | solution.py:22
  26.5 121.0 %all-reduce.3.cloned.1.call-start = ((), (), s32[]{:S(2)}) async-start(), calls=%async_computation.3 | async-start | bytes 262144 | tf_op jit(solution)/shard_map/psum | solution.py:41
  26.6 0.7 copy-start.3
  75.4 0.7 copy-start.4
  76.6 0.9 copy-start.2
  78.6 102.0 %all-reduce.5.cloned.1.call-start = ((), (), s32[]{:S(2)}) async-start(), calls=%async_computation.4 | async-start | bytes 262144 | tf_op jit(solution)/shard_map/psum | solution.py:41
Sparse Core Ops, SparseCore 0:
  11.6 61.1 all-gather.1
  78.7 68.7 all-reduce.2
  149.9 30.6 all-reduce.4

commit v2 on v0

--- a/solution.py
+++ b/solution.py
@@ -38,7 +38,7 @@
     masked_grad = cotangent.astype(jnp.float32) * train_mask.astype(jnp.float32)[:, None]
     delta = backward(masked_grad)[0]
     local_grad = jnp.dot(mixed.T, delta, precision=lax.Precision.HIGHEST)
-    weight_grad = lax.psum(local_grad, ("grp", "blk"))
+    weight_grad = jnp.sum(lax.all_gather(local_grad, ("grp", "blk")), axis=0)
     return (hidden.astype(jnp.bfloat16), weight_grad)
 
 

time: 209 us -> 149 us (0.71)
  waiting for transfers between devices: 167 us -> 106 us
  other arithmetic: 1.51 us -> 5.27 us
  local copies, waits for them, and re-layouts: 6.49 us -> 3.73 us
    psum x1 -> x0, waiting for transfers between devices: 122 us -> none  [shards(): weight_grad = lax.psum(local_grad, ('grp', 'blk'))]
    all_gather x0 -> x1, waiting for transfers between devices: none -> 61.2 us  [shards(): weight_grad = jnp.sum(lax.all_gather(local_grad, ('grp', 'blk')), axis=0)]
    unnamed x11 -> x6, local copies, waits for them, and re-layouts: 3.43 us -> 0.02 us
    reduce_sum x0 -> x1, other arithmetic: none -> 3.1 us  [shards(): weight_grad = jnp.sum(lax.all_gather(local_grad, ('grp', 'blk')), axis=0)]
  transfers between devices with their start and end apart: 3 -> 3, of which waited for: 2 -> 2; matrix products, arithmetic and copies ran while one was open for 1% -> 2% of each run, Pallas kernels for 0% -> 0%
where the time goes in v2:
time: 149 us
  waiting for transfers between devices  106 us (71%)
  between operations  14.1 us (9%)
  blocking collectives  13.5 us (9%)
  other arithmetic  5.27 us (4%)
  local copies, waits for them, and re-layouts  3.73 us (3%)
  starting transfers between devices  3.64 us (2%)
  matrix products  2.44 us (2%)
    all_gather x1, waiting for transfers between devices, shards(): weight_grad = jnp.sum(lax.all_gather(local_grad, ('grp', 'blk')), axis=0)  61.2 us
    all_gather x1, waiting for transfers between devices, shards(): everything = lax.all_gather(scaled, ('grp', 'blk'), axis=0, tiled=True)  45.1 us
    all_to_all x1, blocking collectives, shards(): lax.all_to_all(tile_cols, 'blk', split_axis=0, concat_axis=0, tiled=True)  13.5 us
    all_to_all x1, starting transfers between devices, shards(): lax.all_to_all(tiles, 'blk', split_axis=0, concat_axis=0, tiled=True)  3.56 us
    reduce_sum x1, other arithmetic, shards(): weight_grad = jnp.sum(lax.all_gather(local_grad, ('grp', 'blk')), axis=0)  3.1 us
  transfers between devices with their start and end apart: 3, of which 2 were waited for; matrix products, arithmetic and copies ran while one was open for 2% of the time, Pallas kernels for 0%

profile of v2, /device:TPU:0, one launch (start us, length us, event | category | flops | bytes accessed | tf_op | source)
XLA Modules:
  0.0 149.1 jit_solution(6529033812634187178)
XLA Ops:
  7.2 0.0 copy-start
  7.2 0.0 copy-start.2
  7.2 0.0 all-gather.4.cloned.1.call-start
  7.2 1.5 multiply_convert_fusion.1
  8.7 0.0 all-gather.4.cloned.1.call-update
  8.7 0.7 all_to_all.9
  9.5 13.5 %all_to_all.14 = s32[8,4,1]{1,2,0:T(1,128)S(1)} all-to-all(s32[8,4,1]{1,2,0:T(1,128)S(1)} %bitcast.27), channel_id=1, replica_groups=mesh['grp'=4,'blk'=8] {'blk'}, dimensions={0} | all-to-all | bytes 256 | tf_op jit(solution)/shard_map/all_to_all | solution.py:23
  23.0 3.6 %all-to-all-start.1 = ((bf16[32,128,128]{2,1,0:T(8,128)(2,1)}), bf16[32,128,128]{2,1,0:T(8,128)(2,1)S(1)}, u32[]{:S(2)}, u32[]{:S(2)}) async-start(bf16[32,128,128]{2,1,0:T(8,128)(2,1)} %param.11), calls=%async_computation.1 | async-start | bytes 2097152 | tf_op jit(solution)/shard_map/all_to_all | solution.py:22
  26.5 0.0 copy-start.1
  26.5 0.0 all-gather.6.cloned.1.call-start
  26.6 0.7 convert_element_type.20
  27.3 0.1 add.80
  27.4 0.1 copy.17
  27.5 0.1 copy.18
  27.6 0.1 mul.98
  27.7 45.1 %all-gather.4.cloned.1.call-done = bf16[4096,128]{1,0:T(8,128)(2,1)} async-done(((bf16[128,128]{1,0:T(8,128)(2,1)}), bf16[4096,128]{1,0:T(8,128)(2,1)}) %all-gather.4.cloned.1.call-update) | async-done | bytes 1048592 | tf_op jit(solution)/shard_map/all_gather | solution.py:25
  72.8 2.0 %gather_fusion = bf16[32,128,128]{2,1,0:T(8,128)(2,1)S(1)} fusion(bf16[32,128,128]{2,1,0:T(8,128)(2,1)} %bitcast.24, s32[1024]{0:T(1024)S(1)} %pad_clamp_fusion), kind=kCustom, calls=%fused_computation | custom fusion | bytes 2097280 | tf_op jit(solution)/shard_map/jit(_take)/gather | solution.py:30
  74.8 0.7 copy.19
  75.5 0.0 all-to-all-done.1
  75.5 0.0 copy-done.2
  75.5 0.5 fusion
  76.0 0.0 copy-done
  76.0 0.9 multiply_convert_fusion
  76.9 0.0 copy-done.1
  76.9 1.0 fusion.10
  77.9 0.0 all-gather.6.cloned.1.call-update
  78.0 61.2 %all-gather.6.cloned.1.call-done = f32[4096,256]{1,0:T(8,128)} async-done(((f32[128,256]{1,0:T(8,128)}), f32[4096,256]{1,0:T(8,128)}) %all-gather.6.cloned.1.call-update) | async-done | bytes 4194320 | tf_op jit(solution)/shard_map/all_gather | solution.py:41
  139.2 3.1 %reduce_sum.9 = f32[128,256]{1,0:T(8,128)} reduce(f32[32,128,256]{2,1,0:T(8,128)} %bitcast.23, f32[]{:T(128)} %constant.57.clone.1), dimensions={0}, to_apply=%region_0.1 | reduce | flops 1015808 | bytes 4325380 | tf_op jit(solution)/shard_map/reduce_sum | solution.py:41
  (5 shorter events, 0.0 us)
Async XLA Ops:
  7.2 68.8 %copy-start = (bf16[128,256]{1,0:T(8,128)(2,1)S(1)}, bf16[128,256]{1,0:T(8,128)(2,1)}, u32[]{:S(2)}) copy-start(bf16[128,256]{1,0:T(8,128)(2,1)} %param.13) | copy-start | bytes 196612
  7.2 68.3 %copy-start.2 = (f32[128]{0:T(128)S(1)}, f32[128]{0:T(128)}, u32[]{:S(2)}) copy-start(f32[128]{0:T(128)} %param.10) | copy-start | bytes 1540
  7.2 65.6 %all-gather.4.cloned.1.call-start = ((), (), s32[]{:S(2)}) async-start(), calls=%async_computation.2 | async-start | bytes 1081344 | tf_op jit(solution)/shard_map/all_gather | solution.py:25
  23.0 52.5 %all-to-all-start.1 = ((bf16[32,128,128]{2,1,0:T(8,128)(2,1)}), bf16[32,128,128]{2,1,0:T(8,128)(2,1)S(1)}, u32[]{:S(2)}, u32[]{:S(2)}) async-start(bf16[32,128,128]{2,1,0:T(8,128)(2,1)} %param.11), calls=%async_computation.1 | async-start | bytes 2097152 | tf_op jit(solution)/shard_map/all_to_all | solution.py:22
  26.5 50.4 %copy-start.1 = (bf16[128,256]{1,0:T(8,128)(2,1)S(1)}, bf16[128,256]{1,0:T(8,128)(2,1)}, u32[]{:S(2)}) copy-start(bf16[128,256]{1,0:T(8,128)(2,1)} %param.14) | copy-start | bytes 196612
  26.5 112.6 %all-gather.6.cloned.1.call-start = ((), (), s32[]{:S(2)}) async-start(), calls=%async_computation.3 | async-start | bytes 4325376 | tf_op jit(solution)/shard_map/all_gather | solution.py:41
Sparse Core Ops, SparseCore 0:
  11.6 61.1 all-gather.3
  78.1 61.0 all-gather.5
